TPU v7x, 32 devices: a whole 2x2x4 slice. The times are simulated.
32 devices in a mesh: dp: 2 (over x), hst: 4 (over y, core), chip: 4 (over z).
Axes of the slice: x: 2, y: 2, z: 4, core: 2. Of those that a mesh axis runs over, the one named last changes fastest.
Arguments:
- tokens: bfloat16 [512, 8192], P('dp', ('hst', 'chip')), may hold values from -6 to 6
- out_grad: bfloat16 [512, 8192], P('dp', ('hst', 'chip')), may hold values from -6 to 6
- up_blocks: bfloat16 [112, 16, 128, 128], P(('hst', 'chip')), may hold values from -0.125 to 0.125
- up_cols: int32 [112, 16], P(('hst', 'chip')), may hold values from 0 to 63, all different within a row
- down_blocks: bfloat16 [112, 16, 128, 128], P(('hst', 'chip')), may hold values from -0.09375 to 0.09375
- down_cols: int32 [112, 16], P(('hst', 'chip')), may hold values from 0 to 63, all different within a row
Outputs:
- input_grad: bfloat16 [512, 8192], P('dp', ('hst', 'chip'))
- up_grad: float32 [112, 16, 128, 128], P(('hst', 'chip'), None, 'dp')
- down_grad: float32 [112, 16, 128, 128], P(('hst', 'chip'), None, 'dp')
Inputs may be any that keep to these rules, and one draw needn't show every extreme that they name: `up_cols`: each block row names 16 different block columns; every block column is named by some row. `down_cols`: each block row names 16 different block columns; every block column is named by some row.
All inputs are finite; a program needn't handle non-finite values.
Results may differ from a plain program's by a relative error of at most 0.017.
Values may be sent and summed in bfloat16 or wider, within the bound.
A program may use at most 128 MiB of HBM per device.

v0:
```python
import jax
import jax.numpy as jnp
from jax import lax
from jax.sharding import PartitionSpec as P


def local(tokens, out_grad, up_blocks, up_cols, down_blocks, down_cols):
    whole_x, whole_dy = (
        lax.all_gather(tokens, ("hst", "chip"), axis=1, tiled=True),
        lax.all_gather(out_grad, ("hst", "chip"), axis=1, tiled=True),
    )
    tok_rows = whole_x.shape[0]
    block_size = up_blocks.shape[2]
    local_rows = up_blocks.shape[0]
    dblocks = whole_x.shape[1] // block_size
    x_blocks = whole_x.reshape(tok_rows, dblocks, block_size)
    dy_blocks = whole_dy.reshape(tok_rows, dblocks, block_size)
    x_sel = x_blocks[:, up_cols, :]
    dy_sel = dy_blocks[:, down_cols, :]
    pre_act = jnp.einsum("tjkc,jkhc->tjh", x_sel, up_blocks, preferred_element_type=jnp.float32)
    activated = jax.nn.silu(pre_act).astype(jnp.bfloat16)
    down_part = jnp.einsum("tjh,tjkc->jkhc", activated, dy_sel, preferred_element_type=jnp.float32)
    hidden_grad = jnp.einsum(
        "tjkc,jkhc->tjh", dy_sel, down_blocks, preferred_element_type=jnp.float32
    )
    sigmoid_pre = jax.nn.sigmoid(pre_act)
    pre_grad = (hidden_grad * sigmoid_pre * (1.0 + pre_act * (1.0 - sigmoid_pre))).astype(
        jnp.bfloat16
    )
    up_part = jnp.einsum("tjh,tjkc->jkhc", pre_grad, x_sel, preferred_element_type=jnp.float32)
    up_sum, down_sum = (
        lax.psum_scatter(
            up_part.astype(jnp.bfloat16), "dp", scatter_dimension=2, tiled=True
        ).astype(jnp.float32),
        lax.psum_scatter(
            down_part.astype(jnp.bfloat16), "dp", scatter_dimension=2, tiled=True
        ).astype(jnp.float32),
    )
    onehot = (up_cols[:, :, None] == jnp.arange(dblocks, dtype=jnp.int32)[None, None, :]).astype(
        jnp.bfloat16
    )
    dense_up = jnp.einsum(
        "jkb,jkhc->jhbc", onehot, up_blocks, preferred_element_type=jnp.float32
    ).astype(jnp.bfloat16)
    dense_up = dense_up.reshape(local_rows * block_size, dblocks * block_size)
    flat_grad = pre_grad.reshape(tok_rows, local_rows * block_size)
    partial_value = jnp.dot(flat_grad, dense_up, preferred_element_type=jnp.float32)
    summed = lax.psum_scatter(
        partial_value.astype(jnp.bfloat16), ("hst", "chip"), scatter_dimension=1, tiled=True
    )
    return (summed, up_sum, down_sum)


def solution(mesh):
    placed = (
        P("dp", ("hst", "chip")),
        P("dp", ("hst", "chip")),
        P(("hst", "chip"), None, None, None),
        P(("hst", "chip"), None),
        P(("hst", "chip"), None, None, None),
        P(("hst", "chip"), None),
    )
    return jax.shard_map(
        local,
        mesh=mesh,
        in_specs=placed,
        out_specs=(
            P("dp", ("hst", "chip")),
            P(("hst", "chip"), None, "dp", None),
            P(("hst", "chip"), None, "dp", None),
        ),
        check_vma=False,
    )
```

profile of v0, /device:TPU:0, one launch (start us, length us, event | category | flops | bytes accessed | tf_op | source)
XLA Modules:
  0.0 353.4 jit_solution(15198662633239594076)
XLA Ops:
  7.2 0.0 all-gather.5.cloned.1.call-start
  7.2 1.8 copy.44
  9.0 0.0 all-gather.5.cloned.1.call-update
  9.0 0.0 all-gather.3.cloned.1.call-start
  9.1 1.8 copy.40
  10.9 0.0 all-gather.3.cloned.1.call-update
  10.9 0.0 reduce-scatter.6.cloned.1.call-start
  10.9 0.7 compare_select_fusion.1
  11.6 0.1 reshape.25
  11.7 0.7 compare_select_fusion
  12.4 0.1 reshape.33
  12.5 51.4 %all-gather.5.cloned.1.call-done = bf16[256,8192]{0,1:T(8,128)(2,1)} async-done(((bf16[256,512]{0,1:T(8,128)(2,1)}), bf16[256,8192]{0,1:T(8,128)(2,1)}) %all-gather.5.cloned.1.call-update) | async-done | bytes 4194320 | tf_op jit(solution)/shard_map/all_gather | solution.py:9
  63.9 6.4 %copy.45 = bf16[256,64,128]{2,0,1:T(8,128)(2,1)} copy(bf16[256,64,128]{0,2,1:T(8,128)(2,1)} %bitcast.74) | data formatting | bytes 8388608 | tf_op jit(solution)/shard_map/reshape | solution.py:16
  70.2 45.3 %all-gather.3.cloned.1.call-done = bf16[256,8192]{0,1:T(8,128)(2,1)} async-done(((bf16[256,512]{0,1:T(8,128)(2,1)}), bf16[256,8192]{0,1:T(8,128)(2,1)}) %all-gather.3.cloned.1.call-update) | async-done | bytes 4194320 | tf_op jit(solution)/shard_map/all_gather | solution.py:10
  115.6 6.4 %copy.41 = bf16[256,64,128]{2,0,1:T(8,128)(2,1)} copy(bf16[256,64,128]{0,2,1:T(8,128)(2,1)} %bitcast.75) | data formatting | bytes 8388608 | tf_op jit(solution)/shard_map/reshape | solution.py:17
  122.0 8.5 %gather_fusion.1 = bf16[112,256,128]{2,1,0:T(8,128)(2,1)} fusion(bf16[256,64,128]{2,0,1:T(8,128)(2,1)} %copy.45, s32[1024]{0:T(1024)S(1)} %pad_clamp_fusion), kind=kCustom, calls=%fused_computation.1 | custom fusion | bytes 14680512 | tf_op jit(solution)/shard_map/gather | solution.py:18
  130.5 11.3 %copy.46 = bf16[7,16,256,128]{2,3,1,0:T(8,128)(2,1)} copy(bf16[7,16,256,128]{3,2,1,0:T(8,128)(2,1)} %bitcast.67) | data formatting | bytes 14680064 | tf_op jit(solution)/shard_map/gather | solution.py:18
  141.8 8.5 %gather_fusion = bf16[112,256,128]{2,1,0:T(8,128)(2,1)} fusion(bf16[256,64,128]{2,0,1:T(8,128)(2,1)} %copy.41, s32[1024]{0:T(1024)S(1)} %pad_clamp_fusion.1), kind=kCustom, calls=%fused_computation | custom fusion | bytes 14680512 | tf_op jit(solution)/shard_map/gather | solution.py:19
  150.3 0.0 copy-start
  150.3 0.0 copy-start.2
  150.3 0.0 slice-start
  150.3 6.8 %convolution_bitcast_fusion = f32[256,7,128]{0,2,1:T(8,128)S(1)} fusion(bf16[7,16,128,128]{3,2,1,0:T(8,128)(2,1)} %param.8, bf16[256,7,16,128]{3,0,2,1:T(8,128)(2,1)} %bitcast.68), kind=kOutput, calls=%fused_computation.14 | convolution fusion | flops 939524096 | bytes 11927552 | tf_op jit(solution)/shard_map/tjkc,jkhc->tjh/dot_general | solution.py:20
  157.1 0.0 copy-done
  157.1 0.5 copy-done.2
  157.6 0.0 slice-start.1
  157.6 2.5 fusion.17
  160.1 0.0 slice-done
  160.1 0.0 slice-done.1
  160.1 3.9 %convert_bitcast_fusion.1 = bf16[7,16,128,128]{2,3,1,0:T(8,128)(2,1)} fusion(bf16[7,16,256,128]{2,3,1,0:T(8,128)(2,1)S(1)} %bitcast.70, bf16[256,7,128]{0,2,1:T(8,128)(2,1)S(1)} %fusion.17), kind=kOutput, calls=%fused_computation.13 | convolution fusion | flops 941359104 | bytes 11468800 | tf_op jit(solution)/shard_map/tjh,tjkc->jkhc/dot_general | solution.py:30
  164.1 6.5 %copy.50 = bf16[7,16,128,128]{3,1,0,2:T(8,128)(2,1)} copy(bf16[7,16,128,128]{2,3,1,0:T(8,128)(2,1)} %convert_bitcast_fusion.1) | data formatting | bytes 7340032 | tf_op jit(solution)/shard_map/convert_element_type | solution.py:33
  170.6 0.0 reduce-scatter.6.cloned.1.call-update
  170.6 0.2 reduce-scatter.8.cloned.1.call-start
  170.8 11.6 %copy.42 = bf16[7,16,256,128]{2,3,1,0:T(8,128)(2,1)} copy(bf16[7,16,256,128]{3,2,1,0:T(8,128)(2,1)} %bitcast.71) | data formatting | bytes 14680064 | tf_op jit(solution)/shard_map/gather | solution.py:19
  182.4 7.0 %convert_bitcast_fusion = bf16[7,16,128,128]{2,3,1,0:T(8,128)(2,1)} fusion(bf16[7,16,256,128]{2,3,1,0:T(8,128)(2,1)} %copy.42, f32[256,7,128]{0,2,1:T(8,128)S(1)} %convolution_bitcast_fusion), kind=kOutput, calls=%fused_computation.12 | convolution fusion | flops 942505984 | bytes 11927552 | tf_op jit(solution)/shard_map/tjh,tjkc->jkhc/dot_general | solution.py:22
  189.4 0.0 copy-start.1
  189.4 6.6 %copy.52 = bf16[7,16,128,128]{3,1,0,2:T(8,128)(2,1)} copy(bf16[7,16,128,128]{2,3,1,0:T(8,128)(2,1)} %convert_bitcast_fusion) | data formatting | bytes 7340032 | tf_op jit(solution)/shard_map/convert_element_type | solution.py:36
  196.0 0.0 reduce-scatter.8.cloned.1.call-update
  196.0 0.0 reduce-scatter.4.cloned.1.call-start
  196.1 0.0 copy-done.1
  196.1 11.3 %convolution_convert_fusion = bf16[7,64,128,128]{3,1,2,0:T(8,128)(2,1)} fusion(bf16[7,16,128,128]{3,2,1,0:T(8,128)(2,1)} %param.8, s32[7,16]{1,0:T(8,128)S(1)} %copy-done.1), kind=kOutput, calls=%fused_computation.6 | convolution fusion | flops 242228224 | bytes 18350528 | tf_op jit(solution)/shard_map/jkb,jkhc->jhbc/dot_general | solution.py:42
  207.4 17.7 %fusion.3 = bf16[256,8192]{1,0:T(8,128)(2,1)} fusion(bf16[256,896]{0,1:T(8,128)(2,1)S(1)} %bitcast.76, bf16[112,8,64,128]{3,2,1,0:T(8,128)(2,1)} %bitcast.73), kind=kOutput, calls=%fused_computation.5 | convolution fusion | flops 3760193536 | bytes 19333120 | tf_op jit(solution)/shard_map/dot_general | solution.py:47
  225.1 0.0 reduce-scatter.4.cloned.1.call-update
  225.2 0.0 reduce-scatter.6.cloned.1.call-done
  225.2 4.1 %copy.53 = f32[7,16,64,128]{3,2,1,0:T(8,128)} copy(bf16[7,16,64,128]{3,1,0,2:T(8,128)(2,1)} %reduce-scatter.6.cloned.1.call-done) | data formatting | bytes 5505024
  229.3 40.4 %reduce-scatter.8.cloned.1.call-done = bf16[7,16,64,128]{3,1,0,2:T(8,128)(2,1)} async-done(((bf16[7,16,128,128]{3,1,0,2:T(8,128)(2,1)}), bf16[7,16,64,128]{3,1,0,2:T(8,128)(2,1)}) %reduce-scatter.8.cloned.1.call-update) | async-done | bytes 1835024 | tf_op jit(solution)/shard_map/reduce_scatter | solution.py:35
  269.7 3.9 %copy.54 = f32[7,16,64,128]{3,2,1,0:T(8,128)} copy(bf16[7,16,64,128]{3,1,0,2:T(8,128)(2,1)} %reduce-scatter.8.cloned.1.call-done) | data formatting | bytes 5505024
  273.6 73.3 %reduce-scatter.4.cloned.1.call-done = bf16[256,512]{1,0:T(8,128)(2,1)} async-done(((bf16[256,8192]{1,0:T(8,128)(2,1)}), bf16[256,512]{1,0:T(8,128)(2,1)}) %reduce-scatter.4.cloned.1.call-update) | async-done | bytes 262160 | tf_op jit(solution)/shard_map/reduce_scatter | solution.py:48
  (3 shorter events, 0.0 us)
Async XLA Ops:
  7.2 56.7 %all-gather.5.cloned.1.call-start = ((), (), s32[]{:S(2)}) async-start(), calls=%async_computation.4 | async-start | bytes 4456448 | tf_op jit(solution)/shard_map/all_gather | solution.py:9
  9.0 106.6 %all-gather.3.cloned.1.call-start = ((), (), s32[]{:S(2)}) async-start(), calls=%async_computation.3 | async-start | bytes 4456448 | tf_op jit(solution)/shard_map/all_gather | solution.py:10
  10.9 214.3 %reduce-scatter.6.cloned.1.call-start = ((), (), s32[]{:S(2)}) async-start(), calls=%async_computation.6 | async-start | bytes 5505024 | tf_op jit(solution)/shard_map/reduce_scatter | solution.py:32
  150.3 6.8 %copy-start = (bf16[112,256,128]{2,1,0:T(8,128)(2,1)S(1)}, bf16[112,256,128]{2,1,0:T(8,128)(2,1)}, u32[]{:S(2)}) copy-start(bf16[112,256,128]{2,1,0:T(8,128)(2,1)} %gather_fusion) | copy-start | bytes 22020100
  150.3 7.3 %copy-start.2 = (bf16[7,16,128,128]{3,2,1,0:T(8,128)(2,1)S(1)}, bf16[7,16,128,128]{3,2,1,0:T(8,128)(2,1)}, u32[]{:S(2)}) copy-start(bf16[7,16,128,128]{3,2,1,0:T(8,128)(2,1)} %param.10) | copy-start | bytes 11010052
  150.3 9.8 %slice-start = ((s8[7340032]{0:T(1024)(128)(4,1)}), s8[4194304]{0:T(1024)(128)(4,1)S(1)}, s32[]{:S(2)}) async-start(s8[7340032]{0:T(1024)(128)(4,1)} %bitcast.69), calls=%async_computation.8 | async-start | bytes 8388608
  157.6 2.5 slice-start.1
  170.6 99.2 %reduce-scatter.8.cloned.1.call-start = ((), (), s32[]{:S(2)}) async-start(), calls=%async_computation.7 | async-start | bytes 5505024 | tf_op jit(solution)/shard_map/reduce_scatter | solution.py:35
  189.4 6.7 %copy-start.1 = (s32[7,16]{1,0:T(8,128)S(1)}, s32[7,16]{1,0:T(8,128)}, u32[]{:S(2)}) copy-start(s32[7,16]{1,0:T(8,128)} %param.9) | copy-start | bytes 1348
  196.0 150.8 %reduce-scatter.4.cloned.1.call-start = ((), (), s32[]{:S(2)}) async-start(), calls=%async_computation.5 | async-start | bytes 4456448 | tf_op jit(solution)/shard_map/reduce_scatter | solution.py:48
Sparse Core Ops, SparseCore 0:
  10.8 53.0 all-gather.4
  66.7 48.8 all-gather.2
  170.7 47.7 reduce-scatter.5
  220.5 49.1 reduce-scatter.7
  274.0 72.8 reduce-scatter.3
where the time goes:
time: 355 us; the launch traced here: 353 us
  waiting for transfers between devices  210 us (59%)
  local copies, waits for them, and re-layouts  78 us (22%)
  matrix products  49.3 us (14%)
  between operations  13.9 us (4%)
    reduce_scatter x1, waiting for transfers between devices, local(): lax.psum_scatter(partial_value.astype(jnp.bfloat16), ('hst', 'chip'), sca...  73.3 us
    all_gather x1, waiting for transfers between devices, local(): lax.all_gather(tokens, ('hst', 'chip'), axis=1, tiled=True)  51.4 us
    all_gather x1, waiting for transfers between devices, local(): lax.all_gather(out_grad, ('hst', 'chip'), axis=1, tiled=True)  45.3 us
    reduce_scatter x1, waiting for transfers between devices, local(): lax.psum_scatter(down_part.astype(jnp.bfloat16), 'dp', scatter_dimension=...  40.4 us
    gather x2, local copies, waits for them, and re-layouts, local(): dy_sel = dy_blocks[:, down_cols, :]  20 us
    gather x2, local copies, waits for them, and re-layouts, local(): x_sel = x_blocks[:, up_cols, :]  19.8 us
    dot_general x1, matrix products, local(): jnp.dot(flat_grad, dense_up, preferred_element_type=jnp.float32)  17.7 us
    unnamed x14, local copies, waits for them, and re-layouts  12.1 us
  transfers between devices with their start and end apart: 5, of which 4 were waited for; matrix products, arithmetic and copies ran while one was open for 20% of the time, Pallas kernels for 0%

commit v1 on v0

--- a/solution.py
+++ b/solution.py
@@ -4,10 +4,20 @@
 from jax.sharding import PartitionSpec as P
 
 
+def gather_around(x, axis, dim):
+    ways, here, step = (lax.axis_size(axis), lax.axis_index(axis), x.shape[dim])
+    shape = [n * ways if d == dim else n for d, n in enumerate(x.shape)]
+    full = lax.dynamic_update_slice_in_dim(jnp.zeros(shape, x.dtype), x, here * step, axis=dim)
+    for far in range(1, ways):
+        x = lax.ppermute(x, axis, [(d, (d + 1) % ways) for d in range(ways)])
+        full = lax.dynamic_update_slice_in_dim(full, x, (here - far) % ways * step, axis=dim)
+    return full
+
+
 def local(tokens, out_grad, up_blocks, up_cols, down_blocks, down_cols):
     whole_x, whole_dy = (
         lax.all_gather(tokens, ("hst", "chip"), axis=1, tiled=True),
-        lax.all_gather(out_grad, ("hst", "chip"), axis=1, tiled=True),
+        gather_around(out_grad, ("hst", "chip"), 1),
     )
     tok_rows = whole_x.shape[0]
     block_size = up_blocks.shape[2]

time: 355 us -> 415 us (1.17)
  waiting for transfers between devices: 210 us -> 253 us
  local copies, waits for them, and re-layouts: 78 us -> 91.1 us
    ppermute x0 -> x15, waiting for transfers between devices: none -> 143 us  [gather_around(): x = lax.ppermute(x, axis, [(d, (d + 1) % ways) for d in range(ways)])]
    all_gather x1, waiting for transfers between devices: 51.4 us -> 0.01 us  [local(): lax.all_gather(tokens, ('hst', 'chip'), axis=1, tiled=True)]
    all_gather x1 -> x0, waiting for transfers between devices: 45.3 us -> none  [local(): lax.all_gather(out_grad, ('hst', 'chip'), axis=1, tiled=True)]
    reduce_scatter x1, waiting for transfers between devices: 40.4 us -> 0.02 us  [local(): lax.psum_scatter(down_part.astype(jnp.bfloat16), 'dp', scatter_dimension=...]
    reduce_scatter x1, waiting for transfers between devices: 0.02 us -> 36.9 us  [local(): lax.psum_scatter(up_part.astype(jnp.bfloat16), 'dp', scatter_dimension=2,...]
    dynamic_update_slice x0 -> x16, local copies, waits for them, and re-layouts: none -> 11.5 us  [the longest x15 10.8 us: gather_around(): lax.dynamic_update_slice_in_dim(full, x, (here - far) % ways * step, axis...]
    dot_general x1, matrix products: 2.51 us -> 6.84 us  [local(): jnp.einsum('tjkc,jkhc->tjh', dy_sel, down_blocks, preferred_element_type=...]
    unnamed x14 -> x16, local copies, waits for them, and re-layouts: 12.1 us -> 11.5 us
  transfers between devices with their start and end apart: 5 -> 19, of which waited for: 4 -> 17; matrix products, arithmetic and copies ran while one was open for 20% -> 26% of each run, Pallas kernels for 0% -> 0%
where the time goes in v1:
time: 415 us; the launch traced here: 413 us
  waiting for transfers between devices  253 us (61%)
  local copies, waits for them, and re-layouts  91.1 us (22%)
  matrix products  50.4 us (12%)
  between operations  14.2 us (3%)
    ppermute x15, waiting for transfers between devices, gather_around(): x = lax.ppermute(x, axis, [(d, (d + 1) % ways) for d in range(ways)])  143 us
    reduce_scatter x1, waiting for transfers between devices, local(): lax.psum_scatter(partial_value.astype(jnp.bfloat16), ('hst', 'chip'), sca...  73.2 us
    reduce_scatter x1, waiting for transfers between devices, local(): lax.psum_scatter(up_part.astype(jnp.bfloat16), 'dp', scatter_dimension=2,...  36.9 us
    gather x2, local copies, waits for them, and re-layouts, local(): x_sel = x_blocks[:, up_cols, :]  20.1 us
    gather x2, local copies, waits for them, and re-layouts, local(): dy_sel = dy_blocks[:, down_cols, :]  19.7 us
    dot_general x1, matrix products, local(): jnp.dot(flat_grad, dense_up, preferred_element_type=jnp.float32)  17.6 us
    unnamed x16, local copies, waits for them, and re-layouts  11.5 us
    dot_general x1, matrix products, local(): jnp.einsum('jkb,jkhc->jhbc', onehot, up_blocks, preferred_element_type=jn...  11.3 us
  transfers between devices with their start and end apart: 19, of which 17 were waited for; matrix products, arithmetic and copies ran while one was open for 26% of the time, Pallas kernels for 0%

profile of v1, /device:TPU:0, one launch (start us, length us, event | category | flops | bytes accessed | tf_op | source)
XLA Modules:
  0.0 413.2 jit_solution(3387250204908954394)
XLA Ops:
  7.2 0.0 all-gather.2.cloned.1.call-start
  7.2 1.8 copy.45
  9.0 0.0 all-gather.2.cloned.1.call-update
  9.0 0.0 reduce-scatter.8.cloned.1.call-start
  9.1 1.1 copy.40
  10.2 3.1 collective-permute-start
  13.3 8.4 %collective-permute-done = bf16[256,512]{0,1:T(8,128)(2,1)S(1)} collective-permute-done((bf16[256,512]{0,1:T(8,128)(2,1)S(1)}, bf16[256,512]{0,1:T(8,128)(2,1)S(1)}, u32[]{:S(2)}, u32[]{:S(2)}) %collective-permute-start) | collective-permute-done | bytes 262176 | tf_op jit(solution)/shard_map/ppermute | solution.py:12
  21.7 16.8 %collective-permute-done.1 = bf16[256,512]{0,1:T(8,128)(2,1)S(1)} collective-permute-done((bf16[256,512]{0,1:T(8,128)(2,1)S(1)}, bf16[256,512]{0,1:T(8,128)(2,1)S(1)}, u32[]{:S(2)}, u32[]{:S(2)}) %collective-permute-start.1) | collective-permute-done | bytes 262176 | tf_op jit(solution)/shard_map/ppermute | solution.py:12
  38.5 10.9 %collective-permute-done.2 = bf16[256,512]{0,1:T(8,128)(2,1)S(1)} collective-permute-done((bf16[256,512]{0,1:T(8,128)(2,1)S(1)}, bf16[256,512]{0,1:T(8,128)(2,1)S(1)}, u32[]{:S(2)}, u32[]{:S(2)}) %collective-permute-start.2) | collective-permute-done | bytes 262176 | tf_op jit(solution)/shard_map/ppermute | solution.py:12
  49.4 16.5 %collective-permute-done.3 = bf16[256,512]{0,1:T(8,128)(2,1)S(1)} collective-permute-done((bf16[256,512]{0,1:T(8,128)(2,1)S(1)}, bf16[256,512]{0,1:T(8,128)(2,1)S(1)}, u32[]{:S(2)}, u32[]{:S(2)}) %collective-permute-start.3) | collective-permute-done | bytes 262176 | tf_op jit(solution)/shard_map/ppermute | solution.py:12
  65.9 11.7 %collective-permute-done.4 = bf16[256,512]{0,1:T(8,128)(2,1)S(1)} collective-permute-done((bf16[256,512]{0,1:T(8,128)(2,1)S(1)}, bf16[256,512]{0,1:T(8,128)(2,1)S(1)}, u32[]{:S(2)}, u32[]{:S(2)}) %collective-permute-start.4) | collective-permute-done | bytes 262176 | tf_op jit(solution)/shard_map/ppermute | solution.py:12
  77.6 10.8 %collective-permute-done.5 = bf16[256,512]{0,1:T(8,128)(2,1)S(1)} collective-permute-done((bf16[256,512]{0,1:T(8,128)(2,1)S(1)}, bf16[256,512]{0,1:T(8,128)(2,1)S(1)}, u32[]{:S(2)}, u32[]{:S(2)}) %collective-permute-start.5) | collective-permute-done | bytes 262176 | tf_op jit(solution)/shard_map/ppermute | solution.py:12
  88.4 10.2 %collective-permute-done.6 = bf16[256,512]{0,1:T(8,128)(2,1)S(1)} collective-permute-done((bf16[256,512]{0,1:T(8,128)(2,1)S(1)}, bf16[256,512]{0,1:T(8,128)(2,1)S(1)}, u32[]{:S(2)}, u32[]{:S(2)}) %collective-permute-start.6) | collective-permute-done | bytes 262176 | tf_op jit(solution)/shard_map/ppermute | solution.py:12
  98.6 9.6 %collective-permute-done.7 = bf16[256,512]{0,1:T(8,128)(2,1)S(1)} collective-permute-done((bf16[256,512]{0,1:T(8,128)(2,1)S(1)}, bf16[256,512]{0,1:T(8,128)(2,1)S(1)}, u32[]{:S(2)}, u32[]{:S(2)}) %collective-permute-start.7) | collective-permute-done | bytes 262176 | tf_op jit(solution)/shard_map/ppermute | solution.py:12
  108.2 9.0 %collective-permute-done.8 = bf16[256,512]{0,1:T(8,128)(2,1)S(1)} collective-permute-done((bf16[256,512]{0,1:T(8,128)(2,1)S(1)}, bf16[256,512]{0,1:T(8,128)(2,1)S(1)}, u32[]{:S(2)}, u32[]{:S(2)}) %collective-permute-start.8) | collective-permute-done | bytes 262176 | tf_op jit(solution)/shard_map/ppermute | solution.py:12
  117.2 0.7 compare_select_fusion
  117.9 0.1 reshape.33
  118.0 0.1 reshape.25
  118.1 2.2 broadcast_in_dim.11
  120.3 0.7 constant_dynamic-update-slice_fusion.15
  121.0 4.7 %collective-permute-done.9 = bf16[256,512]{0,1:T(8,128)(2,1)S(1)} collective-permute-done((bf16[256,512]{0,1:T(8,128)(2,1)S(1)}, bf16[256,512]{0,1:T(8,128)(2,1)S(1)}, u32[]{:S(2)}, u32[]{:S(2)}) %collective-permute-start.9) | collective-permute-done | bytes 262176 | tf_op jit(solution)/shard_map/ppermute | solution.py:12
  126.0 0.7 constant_dynamic-update-slice_fusion.14
  126.8 0.7 constant_dynamic-update-slice_fusion.13
  127.5 6.7 %collective-permute-done.10 = bf16[256,512]{0,1:T(8,128)(2,1)S(1)} collective-permute-done((bf16[256,512]{0,1:T(8,128)(2,1)S(1)}, bf16[256,512]{0,1:T(8,128)(2,1)S(1)}, u32[]{:S(2)}, u32[]{:S(2)}) %collective-permute-start.10) | collective-permute-done | bytes 262176 | tf_op jit(solution)/shard_map/ppermute | solution.py:12
  134.2 0.7 constant_dynamic-update-slice_fusion.12
  134.9 0.7 constant_dynamic-update-slice_fusion.11
  135.7 0.7 constant_dynamic-update-slice_fusion.10
  136.4 6.3 %collective-permute-done.11 = bf16[256,512]{0,1:T(8,128)(2,1)S(1)} collective-permute-done((bf16[256,512]{0,1:T(8,128)(2,1)S(1)}, bf16[256,512]{0,1:T(8,128)(2,1)S(1)}, u32[]{:S(2)}, u32[]{:S(2)}) %collective-permute-start.11) | collective-permute-done | bytes 262176 | tf_op jit(solution)/shard_map/ppermute | solution.py:12
  142.7 0.7 constant_dynamic-update-slice_fusion.9
  143.4 0.7 constant_dynamic-update-slice_fusion.8
  144.2 0.7 constant_dynamic-update-slice_fusion.7
  144.9 7.2 %collective-permute-done.12 = bf16[256,512]{0,1:T(8,128)(2,1)S(1)} collective-permute-done((bf16[256,512]{0,1:T(8,128)(2,1)S(1)}, bf16[256,512]{0,1:T(8,128)(2,1)S(1)}, u32[]{:S(2)}, u32[]{:S(2)}) %collective-permute-start.12) | collective-permute-done | bytes 262176 | tf_op jit(solution)/shard_map/ppermute | solution.py:12
  152.0 0.7 constant_dynamic-update-slice_fusion.6
  152.7 0.7 constant_dynamic-update-slice_fusion.5
  153.5 0.7 constant_dynamic-update-slice_fusion.4
  154.2 8.1 %collective-permute-done.13 = bf16[256,512]{0,1:T(8,128)(2,1)S(1)} collective-permute-done((bf16[256,512]{0,1:T(8,128)(2,1)S(1)}, bf16[256,512]{0,1:T(8,128)(2,1)S(1)}, u32[]{:S(2)}, u32[]{:S(2)}) %collective-permute-start.13) | collective-permute-done | bytes 262176 | tf_op jit(solution)/shard_map/ppermute | solution.py:12
  162.3 0.7 constant_dynamic-update-slice_fusion.3
  163.0 0.7 constant_dynamic-update-slice_fusion.2
  163.7 0.7 constant_dynamic-update-slice_fusion.1
  164.4 6.3 %collective-permute-done.14 = bf16[256,512]{0,1:T(8,128)(2,1)S(1)} collective-permute-done((bf16[256,512]{0,1:T(8,128)(2,1)S(1)}, bf16[256,512]{0,1:T(8,128)(2,1)S(1)}, u32[]{:S(2)}, u32[]{:S(2)}) %collective-permute-start.14) | collective-permute-done | bytes 262176 | tf_op jit(solution)/shard_map/ppermute | solution.py:12
  170.7 0.7 constant_dynamic-update-slice_fusion
  171.5 6.4 %copy.42 = bf16[256,64,128]{2,0,1:T(8,128)(2,1)} copy(bf16[256,64,128]{0,2,1:T(8,128)(2,1)} %bitcast) | data formatting | bytes 8388608 | tf_op jit(solution)/shard_map/reshape | solution.py:27
  177.8 8.5 %gather_fusion = bf16[112,256,128]{2,1,0:T(8,128)(2,1)} fusion(bf16[256,64,128]{2,0,1:T(8,128)(2,1)} %copy.42, s32[1024]{0:T(1024)S(1)} %pad_clamp_fusion.1), kind=kCustom, calls=%fused_computation | custom fusion | bytes 14680512 | tf_op jit(solution)/shard_map/gather | solution.py:29
  186.3 11.2 %copy.43 = bf16[7,16,256,128]{2,3,1,0:T(8,128)(2,1)} copy(bf16[7,16,256,128]{3,2,1,0:T(8,128)(2,1)} %bitcast.69) | data formatting | bytes 14680064 | tf_op jit(solution)/shard_map/gather | solution.py:29
  197.5 6.4 %copy.46 = bf16[256,64,128]{2,0,1:T(8,128)(2,1)} copy(bf16[256,64,128]{0,2,1:T(8,128)(2,1)} %bitcast.74) | data formatting | bytes 8388608 | tf_op jit(solution)/shard_map/reshape | solution.py:26
  203.9 8.7 %gather_fusion.1 = bf16[112,256,128]{2,1,0:T(8,128)(2,1)} fusion(bf16[256,64,128]{2,0,1:T(8,128)(2,1)} %copy.46, s32[1024]{0:T(1024)S(1)} %pad_clamp_fusion), kind=kCustom, calls=%fused_computation.1 | custom fusion | bytes 14680512 | tf_op jit(solution)/shard_map/gather | solution.py:28
  212.6 6.8 %convolution_bitcast_fusion = f32[256,7,128]{0,2,1:T(8,128)S(1)} fusion(bf16[7,16,128,128]{3,2,1,0:T(8,128)(2,1)} %param.8, bf16[256,7,16,128]{3,0,2,1:T(8,128)(2,1)} %bitcast.67), kind=kOutput, calls=%fused_computation.14 | convolution fusion | flops 939524096 | bytes 11927552 | tf_op jit(solution)/shard_map/tjkc,jkhc->tjh/dot_general | solution.py:30
  219.3 0.9 copy-done.1
  220.3 3.9 convert_bitcast_fusion
  224.2 6.6 %copy.53 = bf16[7,16,128,128]{3,1,0,2:T(8,128)(2,1)} copy(bf16[7,16,128,128]{2,3,1,0:T(8,128)(2,1)} %convert_bitcast_fusion) | data formatting | bytes 7340032 | tf_op jit(solution)/shard_map/convert_element_type | solution.py:46
  230.8 0.0 reduce-scatter.8.cloned.1.call-update
  230.9 0.2 reduce-scatter.6.cloned.1.call-start
  231.1 11.4 %copy.47 = bf16[7,16,256,128]{2,3,1,0:T(8,128)(2,1)} copy(bf16[7,16,256,128]{3,2,1,0:T(8,128)(2,1)} %bitcast.68) | data formatting | bytes 14680064 | tf_op jit(solution)/shard_map/gather | solution.py:28
  242.5 6.8 %fusion.17 = bf16[256,7,128]{0,2,1:T(8,128)(2,1)S(1)} fusion(bf16[7,16,128,128]{3,2,1,0:T(8,128)(2,1)} %param.10, bf16[256,7,16,128]{3,0,2,1:T(8,128)(2,1)} %bitcast.70, f32[256,7,128]{0,2,1:T(8,128)S(1)} %copy-done.2), kind=kOutput, calls=%fused_computation.18 | convolution fusion | flops 941588480 | bytes 12386304 | tf_op jit(solution)/shard_map/tjkc,jkhc->tjh/dot_general | solution.py:33
  249.4 3.9 convert_bitcast_fusion.1
  253.3 6.5 %copy.51 = bf16[7,16,128,128]{3,1,0,2:T(8,128)(2,1)} copy(bf16[7,16,128,128]{2,3,1,0:T(8,128)(2,1)} %convert_bitcast_fusion.1) | data formatting | bytes 7340032 | tf_op jit(solution)/shard_map/convert_element_type | solution.py:43
  259.8 0.0 reduce-scatter.4.cloned.1.call-start
  259.9 11.3 %convolution_convert_fusion = bf16[7,64,128,128]{3,1,2,0:T(8,128)(2,1)} fusion(bf16[7,16,128,128]{3,2,1,0:T(8,128)(2,1)} %param.8, s32[7,16]{1,0:T(8,128)S(1)} %copy-done.3), kind=kOutput, calls=%fused_computation.6 | convolution fusion | flops 242228224 | bytes 18350528 | tf_op jit(solution)/shard_map/jkb,jkhc->jhbc/dot_general | solution.py:52
  271.2 17.6 %fusion.3 = bf16[256,8192]{1,0:T(8,128)(2,1)} fusion(bf16[256,896]{0,1:T(8,128)(2,1)S(1)} %bitcast.75, bf16[112,8,64,128]{3,2,1,0:T(8,128)(2,1)} %bitcast.71), kind=kOutput, calls=%fused_computation.5 | convolution fusion | flops 3760193536 | bytes 19333120 | tf_op jit(solution)/shard_map/dot_general | solution.py:57
  288.8 0.0 reduce-scatter.8.cloned.1.call-done
  288.8 3.9 copy.55
  292.7 36.9 %reduce-scatter.6.cloned.1.call-done = bf16[7,16,64,128]{3,1,0,2:T(8,128)(2,1)} async-done(((bf16[7,16,128,128]{3,1,0,2:T(8,128)(2,1)}), bf16[7,16,64,128]{3,1,0,2:T(8,128)(2,1)}) %reduce-scatter.6.cloned.1.call-update) | async-done | bytes 1835024 | tf_op jit(solution)/shard_map/reduce_scatter | solution.py:42
  329.6 3.9 copy.54
  333.5 73.2 %reduce-scatter.4.cloned.1.call-done = bf16[256,512]{1,0:T(8,128)(2,1)} async-done(((bf16[256,8192]{1,0:T(8,128)(2,1)}), bf16[256,512]{1,0:T(8,128)(2,1)}) %reduce-scatter.4.cloned.1.call-update) | async-done | bytes 262160 | tf_op jit(solution)/shard_map/reduce_scatter | solution.py:58
  (31 shorter events, 0.1 us)
Async XLA Ops:
  7.2 190.3 %all-gather.2.cloned.1.call-start = ((), (), s32[]{:S(2)}) async-start(), calls=%async_computation.3 | async-start | bytes 4456448 | tf_op jit(solution)/shard_map/all_gather | solution.py:19
  9.0 279.8 %reduce-scatter.8.cloned.1.call-start = ((), (), s32[]{:S(2)}) async-start(), calls=%async_computation.6 | async-start | bytes 5505024 | tf_op jit(solution)/shard_map/reduce_scatter | solution.py:45
  10.2 11.5 %collective-permute-start = (bf16[256,512]{0,1:T(8,128)(2,1)S(1)}, bf16[256,512]{0,1:T(8,128)(2,1)S(1)}, u32[]{:S(2)}, u32[]{:S(2)}) collective-permute-start(bf16[256,512]{0,1:T(8,128)(2,1)S(1)} %copy.40), channel_id=1, source_target_pairs={{0,1},{1,2},{2,3},{3,4},{4,5},{5,6},{6,7},{7,8},{8,9},{9,10},{10,1... | collective-permute-start | bytes 786440 | tf_op jit(solution)/shard_map/ppermute | solution.py:12
  21.7 16.8 %collective-permute-start.1 = (bf16[256,512]{0,1:T(8,128)(2,1)S(1)}, bf16[256,512]{0,1:T(8,128)(2,1)S(1)}, u32[]{:S(2)}, u32[]{:S(2)}) collective-permute-start(bf16[256,512]{0,1:T(8,128)(2,1)S(1)} %collective-permute-done), channel_id=1, source_target_pairs={{0,1},{1,2},{2,3},{3,4},{4,5},{5,6},{6,7},{7,8},{8,9},{9,10},{10,1... | collective-permute-start | bytes 786440 | tf_op jit(solution)/shard_map/ppermute | solution.py:12
  38.5 10.9 %collective-permute-start.2 = (bf16[256,512]{0,1:T(8,128)(2,1)S(1)}, bf16[256,512]{0,1:T(8,128)(2,1)S(1)}, u32[]{:S(2)}, u32[]{:S(2)}) collective-permute-start(bf16[256,512]{0,1:T(8,128)(2,1)S(1)} %collective-permute-done.1), channel_id=1, source_target_pairs={{0,1},{1,2},{2,3},{3,4},{4,5},{5,6},{6,7},{7,8},{8,9},{9,10},{10,1... | collective-permute-start | bytes 786440 | tf_op jit(solution)/shard_map/ppermute | solution.py:12
  49.4 16.5 %collective-permute-start.3 = (bf16[256,512]{0,1:T(8,128)(2,1)S(1)}, bf16[256,512]{0,1:T(8,128)(2,1)S(1)}, u32[]{:S(2)}, u32[]{:S(2)}) collective-permute-start(bf16[256,512]{0,1:T(8,128)(2,1)S(1)} %collective-permute-done.2), channel_id=1, source_target_pairs={{0,1},{1,2},{2,3},{3,4},{4,5},{5,6},{6,7},{7,8},{8,9},{9,10},{10,1... | collective-permute-start | bytes 786440 | tf_op jit(solution)/shard_map/ppermute | solution.py:12
  65.9 11.7 %collective-permute-start.4 = (bf16[256,512]{0,1:T(8,128)(2,1)S(1)}, bf16[256,512]{0,1:T(8,128)(2,1)S(1)}, u32[]{:S(2)}, u32[]{:S(2)}) collective-permute-start(bf16[256,512]{0,1:T(8,128)(2,1)S(1)} %collective-permute-done.3), channel_id=1, source_target_pairs={{0,1},{1,2},{2,3},{3,4},{4,5},{5,6},{6,7},{7,8},{8,9},{9,10},{10,1... | collective-permute-start | bytes 786440 | tf_op jit(solution)/shard_map/ppermute | solution.py:12
  77.6 10.8 %collective-permute-start.5 = (bf16[256,512]{0,1:T(8,128)(2,1)S(1)}, bf16[256,512]{0,1:T(8,128)(2,1)S(1)}, u32[]{:S(2)}, u32[]{:S(2)}) collective-permute-start(bf16[256,512]{0,1:T(8,128)(2,1)S(1)} %collective-permute-done.4), channel_id=1, source_target_pairs={{0,1},{1,2},{2,3},{3,4},{4,5},{5,6},{6,7},{7,8},{8,9},{9,10},{10,1... | collective-permute-start | bytes 786440 | tf_op jit(solution)/shard_map/ppermute | solution.py:12
  88.4 10.2 %collective-permute-start.6 = (bf16[256,512]{0,1:T(8,128)(2,1)S(1)}, bf16[256,512]{0,1:T(8,128)(2,1)S(1)}, u32[]{:S(2)}, u32[]{:S(2)}) collective-permute-start(bf16[256,512]{0,1:T(8,128)(2,1)S(1)} %collective-permute-done.5), channel_id=1, source_target_pairs={{0,1},{1,2},{2,3},{3,4},{4,5},{5,6},{6,7},{7,8},{8,9},{9,10},{10,1... | collective-permute-start | bytes 786440 | tf_op jit(solution)/shard_map/ppermute | solution.py:12
  98.6 9.6 %collective-permute-start.7 = (bf16[256,512]{0,1:T(8,128)(2,1)S(1)}, bf16[256,512]{0,1:T(8,128)(2,1)S(1)}, u32[]{:S(2)}, u32[]{:S(2)}) collective-permute-start(bf16[256,512]{0,1:T(8,128)(2,1)S(1)} %collective-permute-done.6), channel_id=1, source_target_pairs={{0,1},{1,2},{2,3},{3,4},{4,5},{5,6},{6,7},{7,8},{8,9},{9,10},{10,1... | collective-permute-start | bytes 786440 | tf_op jit(solution)/shard_map/ppermute | solution.py:12
  108.2 9.0 %collective-permute-start.8 = (bf16[256,512]{0,1:T(8,128)(2,1)S(1)}, bf16[256,512]{0,1:T(8,128)(2,1)S(1)}, u32[]{:S(2)}, u32[]{:S(2)}) collective-permute-start(bf16[256,512]{0,1:T(8,128)(2,1)S(1)} %collective-permute-done.7), channel_id=1, source_target_pairs={{0,1},{1,2},{2,3},{3,4},{4,5},{5,6},{6,7},{7,8},{8,9},{9,10},{10,1... | collective-permute-start | bytes 786440 | tf_op jit(solution)/shard_map/ppermute | solution.py:12
  117.2 8.5 %collective-permute-start.9 = (bf16[256,512]{0,1:T(8,128)(2,1)S(1)}, bf16[256,512]{0,1:T(8,128)(2,1)S(1)}, u32[]{:S(2)}, u32[]{:S(2)}) collective-permute-start(bf16[256,512]{0,1:T(8,128)(2,1)S(1)} %collective-permute-done.8), channel_id=1, source_target_pairs={{0,1},{1,2},{2,3},{3,4},{4,5},{5,6},{6,7},{7,8},{8,9},{9,10},{10,1... | collective-permute-start | bytes 786440 | tf_op jit(solution)/shard_map/ppermute | solution.py:12
  125.7 8.5 %collective-permute-start.10 = (bf16[256,512]{0,1:T(8,128)(2,1)S(1)}, bf16[256,512]{0,1:T(8,128)(2,1)S(1)}, u32[]{:S(2)}, u32[]{:S(2)}) collective-permute-start(bf16[256,512]{0,1:T(8,128)(2,1)S(1)} %collective-permute-done.9), channel_id=1, source_target_pairs={{0,1},{1,2},{2,3},{3,4},{4,5},{5,6},{6,7},{7,8},{8,9},{9,10},{10,1... | collective-permute-start | bytes 786440 | tf_op jit(solution)/shard_map/ppermute | solution.py:12
  134.2 8.5 %collective-permute-start.11 = (bf16[256,512]{0,1:T(8,128)(2,1)S(1)}, bf16[256,512]{0,1:T(8,128)(2,1)S(1)}, u32[]{:S(2)}, u32[]{:S(2)}) collective-permute-start(bf16[256,512]{0,1:T(8,128)(2,1)S(1)} %collective-permute-done.10), channel_id=1, source_target_pairs={{0,1},{1,2},{2,3},{3,4},{4,5},{5,6},{6,7},{7,8},{8,9},{9,10},{10,1... | collective-permute-start | bytes 786440 | tf_op jit(solution)/shard_map/ppermute | solution.py:12
  142.7 9.3 %collective-permute-start.12 = (bf16[256,512]{0,1:T(8,128)(2,1)S(1)}, bf16[256,512]{0,1:T(8,128)(2,1)S(1)}, u32[]{:S(2)}, u32[]{:S(2)}) collective-permute-start(bf16[256,512]{0,1:T(8,128)(2,1)S(1)} %collective-permute-done.11), channel_id=1, source_target_pairs={{0,1},{1,2},{2,3},{3,4},{4,5},{5,6},{6,7},{7,8},{8,9},{9,10},{10,1... | collective-permute-start | bytes 786440 | tf_op jit(solution)/shard_map/ppermute | solution.py:12
  152.0 10.2 %collective-permute-start.13 = (bf16[256,512]{0,1:T(8,128)(2,1)S(1)}, bf16[256,512]{0,1:T(8,128)(2,1)S(1)}, u32[]{:S(2)}, u32[]{:S(2)}) collective-permute-start(bf16[256,512]{0,1:T(8,128)(2,1)S(1)} %collective-permute-done.12), channel_id=1, source_target_pairs={{0,1},{1,2},{2,3},{3,4},{4,5},{5,6},{6,7},{7,8},{8,9},{9,10},{10,1... | collective-permute-start | bytes 786440 | tf_op jit(solution)/shard_map/ppermute | solution.py:12
  162.2 8.5 %collective-permute-start.14 = (bf16[256,512]{0,1:T(8,128)(2,1)S(1)}, bf16[256,512]{0,1:T(8,128)(2,1)S(1)}, u32[]{:S(2)}, u32[]{:S(2)}) collective-permute-start(bf16[256,512]{0,1:T(8,128)(2,1)S(1)} %collective-permute-done.13), channel_id=1, source_target_pairs={{0,1},{1,2},{2,3},{3,4},{4,5},{5,6},{6,7},{7,8},{8,9},{9,10},{10,1... | collective-permute-start | bytes 786440 | tf_op jit(solution)/shard_map/ppermute | solution.py:12
  203.9 16.4 %slice-start = ((s8[7340032]{0:T(1024)(128)(4,1)}), s8[3145728]{0:T(1024)(128)(4,1)S(1)}, s32[]{:S(2)}) async-start(s8[7340032]{0:T(1024)(128)(4,1)} %bitcast.72), calls=%async_computation.7 | async-start | bytes 6291456
  212.6 7.7 %slice-start.1 = ((s8[7340032]{0:T(1024)(128)(4,1)}), s8[4194304]{0:T(1024)(128)(4,1)S(1)}, s32[]{:S(2)}) async-start(s8[7340032]{0:T(1024)(128)(4,1)} %bitcast.72), calls=%async_computation.8 | async-start | bytes 8388608
  219.3 0.9 copy-start.1
  230.9 98.7 %reduce-scatter.6.cloned.1.call-start = ((), (), s32[]{:S(2)}) async-start(), calls=%async_computation.5 | async-start | bytes 5505024 | tf_op jit(solution)/shard_map/reduce_scatter | solution.py:42
  231.1 11.4 %copy-start.2 = (f32[256,7,128]{0,2,1:T(8,128)S(1)}, f32[256,7,128]{0,2,1:T(8,128)}, u32[]{:S(2)}) copy-start(f32[256,7,128]{0,2,1:T(8,128)} %copy-done.1) | copy-start | bytes 2752516
  242.5 6.9 %copy-start = (bf16[7,16,256,128]{2,3,1,0:T(8,128)(2,1)S(1)}, bf16[7,16,256,128]{2,3,1,0:T(8,128)(2,1)}, u32[]{:S(2)}) copy-start(bf16[7,16,256,128]{2,3,1,0:T(8,128)(2,1)} %copy.47) | copy-start | bytes 22020100
  253.3 6.6 %copy-start.3 = (s32[7,16]{1,0:T(8,128)S(1)}, s32[7,16]{1,0:T(8,128)}, u32[]{:S(2)}) copy-start(s32[7,16]{1,0:T(8,128)} %param.9) | copy-start | bytes 1348
  259.8 146.8 %reduce-scatter.4.cloned.1.call-start = ((), (), s32[]{:S(2)}) async-start(), calls=%async_computation.4 | async-start | bytes 4456448 | tf_op jit(solution)/shard_map/reduce_scatter | solution.py:58
Sparse Core Ops, SparseCore 0:
  10.8 61.8 all-gather.1
  231.0 46.5 reduce-scatter.7
  280.4 49.1 reduce-scatter.5
  333.9 72.7 reduce-scatter.3
